TPU v7x, 256 devices: a whole 4x4x8 slice. The times are simulated.
256 devices in a mesh: energy: 64 (over z, x, y_lo), mom: 4 (over y_hi, core).
Axes of the slice: x: 4, y: 4 (y_hi: 2, y_lo: 2; y = y_hi * 2 + y_lo), z: 8, core: 2. Of those that a mesh axis runs over, the one named last changes fastest.
Arguments:
- green: bfloat16 [4, 128, 16, 2048], P('mom', 'energy'), may hold values from -6 to 6
- coupling: float32 [4, 6, 9, 5, 16], P('mom'), may hold values from -0.12 to 0.12
- gradient: bfloat16 [5, 3, 16, 1024], replicated, may hold values from -1 to 1
- neighbours: int32 [16, 5], replicated, may hold values from 0 to 15, as said below
- offsets: int32 [3], replicated, may hold values from 1 to 4, as said below
Outputs:
- sigma: float32 [128, 16, 2048], P('energy', 'mom')
Inputs may be any that keep to these rules, and one draw needn't show every extreme that they name: `neighbours`: each row names 5 different atoms, none of them the row's own atom. `offsets`: one offset is at most 2 and one equals 4.
All inputs are finite; a program needn't handle non-finite values.
Results may differ from a plain program's by a relative error of at most 0.012.
Values may be sent and summed in bfloat16 or wider, within the bound.
A program may use at most 64 MiB of HBM per device.

v0:
```python
import jax
import jax.numpy as jnp
from jax import lax
from jax.sharding import PartitionSpec as P

NO = 32
NB = 5
NW = 3


def shifted_2(array, axis, by):
    length = lax.axis_size(axis)
    pairs = [(i, i + by) for i in range(length) if 0 <= i + by < length]
    return lax.ppermute(array, axis, pairs)


def split_up(array, dim, length):
    before, after = (array.shape[:dim], array.shape[dim + 1 :])
    return jnp.moveaxis(array.reshape(*before, length, -1, *after), dim, 0)


def sum_at_owner(array, axis, dim):
    length = lax.axis_size(axis)
    blocks = lax.all_to_all(split_up(array, dim, length), axis, 0, 0, tiled=True)
    return jnp.sum(blocks, axis=0)


def shifted_stack(window, offsets, count, margin):
    pieces = []
    for phonon in range(NW):
        for direction in (1, -1):
            start = margin - direction * offsets[phonon]
            pieces.append(lax.dynamic_slice_in_dim(window, start, count, 0))
    return jnp.stack(pieces, 0)


def sandwich(shifted, weights, gradient, neighbours):
    count = shifted.shape[1]
    natoms = shifted.shape[2]
    blocks = shifted.reshape(2 * NW, count, natoms, 2, NO, NO)

    def one_slot(total, slot):
        table = lax.dynamic_index_in_dim(weights, slot, 2, keepdims=False).reshape(
            2 * NW, 3, 3, natoms
        )
        derivs = lax.dynamic_index_in_dim(gradient, slot, 0, keepdims=False).reshape(
            3, natoms, NO, NO
        )
        kernel = jnp.einsum("sija,janl->aslin", table, derivs.astype(jnp.float32)).astype(
            jnp.bfloat16
        )
        column = lax.dynamic_index_in_dim(neighbours, slot, 1, keepdims=False)
        gathered = jnp.take(blocks, column, axis=2)
        middle = jnp.einsum(
            "seacml,aslin->aiecmn", gathered, kernel, preferred_element_type=jnp.float32
        ).astype(jnp.bfloat16)
        total = total + jnp.einsum(
            "iapm,aiecmn->eacpn", derivs, middle, preferred_element_type=jnp.float32
        )
        return (total, None)

    start_total = jnp.zeros((count, natoms, 2, NO, NO), jnp.float32)
    total, _ = lax.scan(one_slot, start_total, jnp.arange(NB, dtype=jnp.int32))
    return total


def body(green, coupling, gradient, neighbours, offsets):
    local_block = green[0]
    count = local_block.shape[0]
    natoms = local_block.shape[1]
    below_first = shifted_2(local_block, "energy", 1)
    below_second = shifted_2(local_block, "energy", 2)
    above_first = shifted_2(local_block, "energy", -1)
    above_second = shifted_2(local_block, "energy", -2)
    window = jnp.concatenate(
        [below_second, below_first, local_block, above_first, above_second], axis=0
    )
    shifted = shifted_stack(window, offsets, count, 2 * count)
    partial_terms = sandwich(shifted, coupling[0], gradient, neighbours).reshape(
        count, natoms, 2 * NO * NO
    )
    return sum_at_owner(partial_terms, "mom", 1)


def solution(mesh):
    in_specs = (P("mom", "energy", None, None), P("mom", None, None, None, None), P(), P(), P())
    out_specs = P("energy", "mom", None)
    return jax.shard_map(body, mesh=mesh, in_specs=in_specs, out_specs=out_specs, check_vma=False)
```

profile of v0, /device:TPU:129, one launch (start us, length us, event | category | flops | bytes accessed | tf_op | source)
XLA Modules:
  0.0 155.5 jit_solution(7183389722900616051)
XLA Ops:
  0.0 3.1 %collective-permute-start = (bf16[2,16,2048]{2,1,0:T(8,128)(2,1)}, bf16[2,16,2048]{2,1,0:T(8,128)(2,1)S(1)}, u32[]{:S(2)}, u32[]{:S(2)}) collective-permute-start(bf16[2,16,2048]{2,1,0:T(8,128)(2,1)} %bitcast.94), channel_id=1, source_target_pairs={{0,8},{4,12},{8,16},{12,20},{16,24},{20,28},{24,32},{28,36},{32,40... | collective-permute-start | bytes 393224 | tf_op jit(solution)/shard_map/ppermute | solution.py:14
  3.1 5.5 %collective-permute-start.3 = (bf16[2,16,2048]{2,1,0:T(8,128)(2,1)}, bf16[2,16,2048]{2,1,0:T(8,128)(2,1)S(1)}, u32[]{:S(2)}, u32[]{:S(2)}) collective-permute-start(bf16[2,16,2048]{2,1,0:T(8,128)(2,1)} %bitcast.95), channel_id=1, source_target_pairs={{8,0},{12,4},{16,8},{20,12},{24,16},{28,20},{32,24},{36,28},{40,32... | collective-permute-start | bytes 393224 | tf_op jit(solution)/shard_map/ppermute | solution.py:14
  8.6 2.9 %collective-permute-start.2 = (bf16[2,16,2048]{2,1,0:T(8,128)(2,1)}, bf16[2,16,2048]{2,1,0:T(8,128)(2,1)S(1)}, u32[]{:S(2)}, u32[]{:S(2)}) collective-permute-start(bf16[2,16,2048]{2,1,0:T(8,128)(2,1)} %bitcast.96), channel_id=1, source_target_pairs={{4,0},{8,4},{12,8},{16,12},{20,16},{24,20},{28,24},{32,28},{36,32}... | collective-permute-start | bytes 393224 | tf_op jit(solution)/shard_map/ppermute | solution.py:14
  11.6 2.4 %collective-permute-start.1 = (bf16[2,16,2048]{2,1,0:T(8,128)(2,1)}, bf16[2,16,2048]{2,1,0:T(8,128)(2,1)S(1)}, u32[]{:S(2)}, u32[]{:S(2)}) collective-permute-start(bf16[2,16,2048]{2,1,0:T(8,128)(2,1)} %bitcast.97), channel_id=1, source_target_pairs={{0,4},{4,8},{8,12},{12,16},{16,20},{20,24},{24,28},{28,32},{32,36}... | collective-permute-start | bytes 393224 | tf_op jit(solution)/shard_map/ppermute | solution.py:14
  13.9 1.4 fusion.25
  21.1 1.6 %copy.64 = bf16[1,6,9,5,16]{4,1,3,2,0:T(8,128)(2,1)} copy(f32[1,6,9,5,16]{4,0,3,2,1:T(1,128)} %param.8) | data formatting | bytes 25920 | tf_op args[1]
  36.4 103.7 %while.11 = (s32[]{:T(128)}, f32[2,16,2,32,32]{3,4,2,0,1:T(8,128)}, s32[5]{0:T(128)S(1)}, bf16[5,3,16,1024]{3,2,1,0:T(8,128)(2,1)}, bf16[6,9,5,16]{3,0,2,1:T(8,1...) while((s32[]{:T(128)}, f32[2,16,2,32,32]{3,4,2,0,1:T(8,128)}, ...), condition=%wide.region_1.2_spmd.clone, body=%wide.region_0.1_spmd.clone.sunk | while | flops 90571880 | bytes 4666257 | solution.py:63
  41.2 1.5 constant_dynamic-slice_fusion.12
  42.7 1.2 reshape.80
  43.9 3.5 %convert_bitcast_fusion.2 = bf16[16,6,32,3,32,1,1]{2,1,3,4,0,6,5:T(8,128)(2,1)} fusion(bf16[6,3,3,16,1]{0,2,1,4,3:T(4,128)(2,1)} %copy.74, bf16[3,16,32,32,1]{3,2,1,0,4:T(8,128)(2,1)S(1)} %bitcast.91), kind=kOutput, calls=%fused_computation.5.clone.1 | convolution fusion | flops 1769472 | bytes 689856 | tf_op jit(solution)/shard_map/while/body/eval_jaxpr/sija,janl->aslin/dot_general | solution.py:49
  47.4 2.6 %gather_fusion = bf16[16,6,2,2,32,32]{5,4,3,2,1,0:T(8,128)(2,1)} fusion(bf16[6,2,16,2,32,32]{5,4,3,2,1,0:T(8,128)(2,1)S(1)} %get-tuple-element.172, s32[1024]{0:T(1024)S(1)} %pad_clamp_fusion.2), kind=kCustom, calls=%fused_computation.clone.clone.1 | custom fusion | bytes 1572928 | tf_op jit(solution)/shard_map/while/body/eval_jaxpr/jit(_take)/gather | solution.py:53
  50.1 7.0 %fusion.43 = f32[2,16,2,32,32]{3,4,2,0,1:T(8,128)} fusion(bf16[16,6,32,3,32,1,1]{2,1,3,4,0,6,5:T(8,128)(2,1)} %convert_bitcast_fusion.2, f32[2,16,2,32,32]{3,4,2,0,1:T(8,128)} %get-tuple-element.157, pred[]{:T(512)S(6)} %compare.3, bf16[16,6,2,2,32,32]{5,4,3,2,1,0:T(8,128)(2,1)} %gather_fusion, pred[16]{0:T(512)(128)(4,1)S(1)} %get-tuple-element.145, ...), kind=kOutput, calls=%fused_computation.10.clone.1 | convolution fusion | flops 88801280 | bytes 1998865 | tf_op jit(solution)/shard_map/while/body/eval_jaxpr/iapm,aiecmn->eacpn/dot_general | solution.py:57
  61.8 1.5 constant_dynamic-slice_fusion.12
  63.3 1.2 reshape.80
  64.5 3.5 %convert_bitcast_fusion.2 = bf16[16,6,32,3,32,1,1]{2,1,3,4,0,6,5:T(8,128)(2,1)} fusion(bf16[6,3,3,16,1]{0,2,1,4,3:T(4,128)(2,1)} %copy.74, bf16[3,16,32,32,1]{3,2,1,0,4:T(8,128)(2,1)S(1)} %bitcast.91), kind=kOutput, calls=%fused_computation.5.clone.1 | convolution fusion | flops 1769472 | bytes 689856 | tf_op jit(solution)/shard_map/while/body/eval_jaxpr/sija,janl->aslin/dot_general | solution.py:49
  68.0 2.6 %gather_fusion = bf16[16,6,2,2,32,32]{5,4,3,2,1,0:T(8,128)(2,1)} fusion(bf16[6,2,16,2,32,32]{5,4,3,2,1,0:T(8,128)(2,1)S(1)} %get-tuple-element.172, s32[1024]{0:T(1024)S(1)} %pad_clamp_fusion.2), kind=kCustom, calls=%fused_computation.clone.clone.1 | custom fusion | bytes 1572928 | tf_op jit(solution)/shard_map/while/body/eval_jaxpr/jit(_take)/gather | solution.py:53
  70.6 7.2 %fusion.43 = f32[2,16,2,32,32]{3,4,2,0,1:T(8,128)} fusion(bf16[16,6,32,3,32,1,1]{2,1,3,4,0,6,5:T(8,128)(2,1)} %convert_bitcast_fusion.2, f32[2,16,2,32,32]{3,4,2,0,1:T(8,128)} %get-tuple-element.157, pred[]{:T(512)S(6)} %compare.3, bf16[16,6,2,2,32,32]{5,4,3,2,1,0:T(8,128)(2,1)} %gather_fusion, pred[16]{0:T(512)(128)(4,1)S(1)} %get-tuple-element.145, ...), kind=kOutput, calls=%fused_computation.10.clone.1 | convolution fusion | flops 88801280 | bytes 1998865 | tf_op jit(solution)/shard_map/while/body/eval_jaxpr/iapm,aiecmn->eacpn/dot_general | solution.py:57
  82.5 1.5 constant_dynamic-slice_fusion.12
  84.1 1.2 reshape.80
  85.3 3.5 %convert_bitcast_fusion.2 = bf16[16,6,32,3,32,1,1]{2,1,3,4,0,6,5:T(8,128)(2,1)} fusion(bf16[6,3,3,16,1]{0,2,1,4,3:T(4,128)(2,1)} %copy.74, bf16[3,16,32,32,1]{3,2,1,0,4:T(8,128)(2,1)S(1)} %bitcast.91), kind=kOutput, calls=%fused_computation.5.clone.1 | convolution fusion | flops 1769472 | bytes 689856 | tf_op jit(solution)/shard_map/while/body/eval_jaxpr/sija,janl->aslin/dot_general | solution.py:49
  88.8 2.6 %gather_fusion = bf16[16,6,2,2,32,32]{5,4,3,2,1,0:T(8,128)(2,1)} fusion(bf16[6,2,16,2,32,32]{5,4,3,2,1,0:T(8,128)(2,1)S(1)} %get-tuple-element.172, s32[1024]{0:T(1024)S(1)} %pad_clamp_fusion.2), kind=kCustom, calls=%fused_computation.clone.clone.1 | custom fusion | bytes 1572928 | tf_op jit(solution)/shard_map/while/body/eval_jaxpr/jit(_take)/gather | solution.py:53
  91.4 7.2 %fusion.43 = f32[2,16,2,32,32]{3,4,2,0,1:T(8,128)} fusion(bf16[16,6,32,3,32,1,1]{2,1,3,4,0,6,5:T(8,128)(2,1)} %convert_bitcast_fusion.2, f32[2,16,2,32,32]{3,4,2,0,1:T(8,128)} %get-tuple-element.157, pred[]{:T(512)S(6)} %compare.3, bf16[16,6,2,2,32,32]{5,4,3,2,1,0:T(8,128)(2,1)} %gather_fusion, pred[16]{0:T(512)(128)(4,1)S(1)} %get-tuple-element.145, ...), kind=kOutput, calls=%fused_computation.10.clone.1 | convolution fusion | flops 88801280 | bytes 1998865 | tf_op jit(solution)/shard_map/while/body/eval_jaxpr/iapm,aiecmn->eacpn/dot_general | solution.py:57
  103.3 1.5 constant_dynamic-slice_fusion.12
  106.1 3.5 %convert_bitcast_fusion.2 = bf16[16,6,32,3,32,1,1]{2,1,3,4,0,6,5:T(8,128)(2,1)} fusion(bf16[6,3,3,16,1]{0,2,1,4,3:T(4,128)(2,1)} %copy.74, bf16[3,16,32,32,1]{3,2,1,0,4:T(8,128)(2,1)S(1)} %bitcast.91), kind=kOutput, calls=%fused_computation.5.clone.1 | convolution fusion | flops 1769472 | bytes 689856 | tf_op jit(solution)/shard_map/while/body/eval_jaxpr/sija,janl->aslin/dot_general | solution.py:49
  109.6 2.6 %gather_fusion = bf16[16,6,2,2,32,32]{5,4,3,2,1,0:T(8,128)(2,1)} fusion(bf16[6,2,16,2,32,32]{5,4,3,2,1,0:T(8,128)(2,1)S(1)} %get-tuple-element.172, s32[1024]{0:T(1024)S(1)} %pad_clamp_fusion.2), kind=kCustom, calls=%fused_computation.clone.clone.1 | custom fusion | bytes 1572928 | tf_op jit(solution)/shard_map/while/body/eval_jaxpr/jit(_take)/gather | solution.py:53
  112.2 7.2 %fusion.43 = f32[2,16,2,32,32]{3,4,2,0,1:T(8,128)} fusion(bf16[16,6,32,3,32,1,1]{2,1,3,4,0,6,5:T(8,128)(2,1)} %convert_bitcast_fusion.2, f32[2,16,2,32,32]{3,4,2,0,1:T(8,128)} %get-tuple-element.157, pred[]{:T(512)S(6)} %compare.3, bf16[16,6,2,2,32,32]{5,4,3,2,1,0:T(8,128)(2,1)} %gather_fusion, pred[16]{0:T(512)(128)(4,1)S(1)} %get-tuple-element.145, ...), kind=kOutput, calls=%fused_computation.10.clone.1 | convolution fusion | flops 88801280 | bytes 1998865 | tf_op jit(solution)/shard_map/while/body/eval_jaxpr/iapm,aiecmn->eacpn/dot_general | solution.py:57
  124.1 1.5 constant_dynamic-slice_fusion.12
  126.9 3.5 %convert_bitcast_fusion.2 = bf16[16,6,32,3,32,1,1]{2,1,3,4,0,6,5:T(8,128)(2,1)} fusion(bf16[6,3,3,16,1]{0,2,1,4,3:T(4,128)(2,1)} %copy.74, bf16[3,16,32,32,1]{3,2,1,0,4:T(8,128)(2,1)S(1)} %bitcast.91), kind=kOutput, calls=%fused_computation.5.clone.1 | convolution fusion | flops 1769472 | bytes 689856 | tf_op jit(solution)/shard_map/while/body/eval_jaxpr/sija,janl->aslin/dot_general | solution.py:49
  130.3 2.6 %gather_fusion = bf16[16,6,2,2,32,32]{5,4,3,2,1,0:T(8,128)(2,1)} fusion(bf16[6,2,16,2,32,32]{5,4,3,2,1,0:T(8,128)(2,1)S(1)} %get-tuple-element.172, s32[1024]{0:T(1024)S(1)} %pad_clamp_fusion.2), kind=kCustom, calls=%fused_computation.clone.clone.1 | custom fusion | bytes 1572928 | tf_op jit(solution)/shard_map/while/body/eval_jaxpr/jit(_take)/gather | solution.py:53
  133.0 7.2 %fusion.43 = f32[2,16,2,32,32]{3,4,2,0,1:T(8,128)} fusion(bf16[16,6,32,3,32,1,1]{2,1,3,4,0,6,5:T(8,128)(2,1)} %convert_bitcast_fusion.2, f32[2,16,2,32,32]{3,4,2,0,1:T(8,128)} %get-tuple-element.157, pred[]{:T(512)S(6)} %compare.3, bf16[16,6,2,2,32,32]{5,4,3,2,1,0:T(8,128)(2,1)} %gather_fusion, pred[16]{0:T(512)(128)(4,1)S(1)} %get-tuple-element.145, ...), kind=kOutput, calls=%fused_computation.10.clone.1 | convolution fusion | flops 88801280 | bytes 1998865 | tf_op jit(solution)/shard_map/while/body/eval_jaxpr/iapm,aiecmn->eacpn/dot_general | solution.py:57
  140.2 1.6 copy.24
  142.2 12.5 %all_to_all.5 = f32[4,2,4,2048]{3,2,1,0:T(4,128)S(1)} all-to-all(f32[4,2,4,2048]{3,2,1,0:T(4,128)S(1)} %copy.25), channel_id=1, replica_groups=mesh['energy'=64,'mom'=4] {'mom'}, dimensions={0} | all-to-all | bytes 524288 | tf_op jit(solution)/shard_map/all_to_all | solution.py:24
  (56 shorter events, 31.2 us)
Async XLA Ops:
  0.0 22.6 %collective-permute-start = (bf16[2,16,2048]{2,1,0:T(8,128)(2,1)}, bf16[2,16,2048]{2,1,0:T(8,128)(2,1)S(1)}, u32[]{:S(2)}, u32[]{:S(2)}) collective-permute-start(bf16[2,16,2048]{2,1,0:T(8,128)(2,1)} %bitcast.94), channel_id=1, source_target_pairs={{0,8},{4,12},{8,16},{12,20},{16,24},{20,28},{24,32},{28,36},{32,40... | collective-permute-start | bytes 393224 | tf_op jit(solution)/shard_map/ppermute | solution.py:14
  3.1 20.5 %collective-permute-start.3 = (bf16[2,16,2048]{2,1,0:T(8,128)(2,1)}, bf16[2,16,2048]{2,1,0:T(8,128)(2,1)S(1)}, u32[]{:S(2)}, u32[]{:S(2)}) collective-permute-start(bf16[2,16,2048]{2,1,0:T(8,128)(2,1)} %bitcast.95), channel_id=1, source_target_pairs={{8,0},{12,4},{16,8},{20,12},{24,16},{28,20},{32,24},{36,28},{40,32... | collective-permute-start | bytes 393224 | tf_op jit(solution)/shard_map/ppermute | solution.py:14
  8.6 15.0 %collective-permute-start.2 = (bf16[2,16,2048]{2,1,0:T(8,128)(2,1)}, bf16[2,16,2048]{2,1,0:T(8,128)(2,1)S(1)}, u32[]{:S(2)}, u32[]{:S(2)}) collective-permute-start(bf16[2,16,2048]{2,1,0:T(8,128)(2,1)} %bitcast.96), channel_id=1, source_target_pairs={{4,0},{8,4},{12,8},{16,12},{20,16},{24,20},{28,24},{32,28},{36,32}... | collective-permute-start | bytes 393224 | tf_op jit(solution)/shard_map/ppermute | solution.py:14
  11.6 11.1 %collective-permute-start.1 = (bf16[2,16,2048]{2,1,0:T(8,128)(2,1)}, bf16[2,16,2048]{2,1,0:T(8,128)(2,1)S(1)}, u32[]{:S(2)}, u32[]{:S(2)}) collective-permute-start(bf16[2,16,2048]{2,1,0:T(8,128)(2,1)} %bitcast.97), channel_id=1, source_target_pairs={{0,4},{4,8},{8,12},{12,16},{16,20},{20,24},{24,28},{28,32},{32,36}... | collective-permute-start | bytes 393224 | tf_op jit(solution)/shard_map/ppermute | solution.py:14
  30.7 3.4 %copy-start = (bf16[1,2,16,2,32,32]{5,4,3,2,1,0:T(8,128)(2,1)S(1)}, bf16[1,2,16,2,32,32]{5,4,3,2,1,0:T(8,128)(2,1)}, u32[]{:S(2)}) copy-start(bf16[1,2,16,2,32,32]{5,4,3,2,1,0:T(8,128)(2,1)} %stack.24) | copy-start | bytes 393220
where the time goes:
time: 159 us; the launch traced here: 155 us
  local copies, waits for them, and re-layouts  55.9 us (35%)
  matrix products  53.2 us (33%)
  starting transfers between devices  13.9 us (9%)
  blocking collectives  12.5 us (8%)
  loops' own time  9.8 us (6%)
  between operations  5.93 us (4%)
  other arithmetic  4.22 us (3%)
    dot_general x5, matrix products, one_slot(): jnp.einsum('iapm,aiecmn->eacpn', derivs, middle, preferred_element_type=j...  35.8 us
    dot_general x5, matrix products, one_slot(): jnp.einsum('sija,janl->aslin', table, derivs.astype(jnp.float32))  17.4 us
    ppermute x4, starting transfers between devices, shifted_2(): return lax.ppermute(array, axis, pairs)  13.9 us
    gather x5, local copies, waits for them, and re-layouts, one_slot(): gathered = jnp.take(blocks, column, axis=2)  13.2 us
    all_to_all x1, blocking collectives, sum_at_owner(): lax.all_to_all(split_up(array, dim, length), axis, 0, 0, tiled=True)  12.5 us
    another operation x1, loops' own time, sandwich(): total, _ = lax.scan(one_slot, start_total, jnp.arange(NB, dtype=jnp.int32))  9.8 us
    another operation x7, local copies, waits for them, and re-layouts, shifted_stack(): return jnp.stack(pieces, 0)  8.12 us
    dynamic_slice x5, local copies, waits for them, and re-layouts, one_slot(): lax.dynamic_index_in_dim(gradient, slot, 0, keepdims=False)  7.68 us
  transfers between devices with their start and end apart: 4, of which 0 were waited for; matrix products, arithmetic and copies ran while one was open for 3% of the time, Pallas kernels for 0%

commit v1 on v0

v1 whole, which is shorter than its diff:
```python
import jax
import jax.numpy as jnp
from jax import lax
from jax.experimental import pallas as pl
from jax.experimental.pallas import tpu as pltpu
from jax.sharding import PartitionSpec as P

NO = 32
NB = 5
NW = 3
NA = 16
NS = 2 * NW
ROWS = NB * 3 * NA
MESH = pl.DeviceIdType.MESH
F32 = jnp.float32
BF16 = jnp.bfloat16
NT = (((1,), (1,)), ((), ()))
SHIFTS = (-2, -1, 1, 2)


def lane_group(rows, lanes=128):
    return lax.broadcasted_iota(jnp.int32, (rows, lanes), 1) // NO


def kernel(
    green, coupling, gradient, neighbours, offsets, out,
    own, halo, grad_v, coup_v, near, offs,
    spread, coef, kern, derivs, wide, blocks, sums, send_buf, recv_buf, turned,
    local_sem, halo_send, halo_recv, part_send, part_recv,
):
    n_energy = lax.axis_size("energy")
    energy = lax.axis_index("energy")
    mom = lax.axis_index("mom")

    loads = [
        pltpu.make_async_copy(gradient, grad_v, local_sem.at[0]),
        pltpu.make_async_copy(coupling, coup_v, local_sem.at[1]),
        pltpu.make_async_copy(offsets, offs, local_sem.at[2]),
        pltpu.make_async_copy(green, own, local_sem.at[3]),
        pltpu.make_async_copy(neighbours, near, local_sem.at[4]),
    ]
    for load in loads:
        load.start()

    def inside(by):
        return jnp.logical_and(energy + by >= 0, energy + by < n_energy)

    barrier = pltpu.get_barrier_semaphore()
    for by in SHIFTS:
        @pl.when(inside(by))
        def _():
            pl.semaphore_signal(barrier, inc=1, device_id={"energy": energy + by}, device_id_type=MESH)
    for step in range(1, 4):
        pl.semaphore_signal(barrier, inc=1, device_id={"mom": lax.rem(mom + step, 4)}, device_id_type=MESH)
    expected = 3
    for by in SHIFTS:
        expected = expected + inside(by).astype(jnp.int32)

    loads[0].wait()
    row = lax.broadcasted_iota(jnp.int32, (128, 512), 0)
    col = lax.broadcasted_iota(jnp.int32, (128, 512), 1)
    pick = jnp.where(
        jnp.logical_and(row // NO == col // 128, row % NO == col % NO), 1.0, 0.0
    ).astype(BF16)

    def spread_chunk(chunk, carry):
        part = grad_v[:, pl.ds(pl.multiple_of(chunk * 128, 128), 128)]
        wide_part = jnp.dot(part, pick, preferred_element_type=F32)
        for q in range(4):
            start = pl.multiple_of((chunk * 4 + q) * ROWS, 8)
            spread[pl.ds(start, ROWS), :] = wide_part[:, q * 128 : (q + 1) * 128]
        return carry

    lax.fori_loop(0, 8, spread_chunk, 0)

    pl.semaphore_wait(barrier, expected)

    def halo_copy(slot):
        by = SHIFTS[slot]
        return pltpu.make_async_remote_copy(
            src_ref=green,
            dst_ref=halo.at[3 - slot],
            send_sem=halo_send.at[slot],
            recv_sem=halo_recv.at[3 - slot],
            device_id={"energy": energy + by},
            device_id_type=MESH,
        )

    for slot in range(4):
        @pl.when(inside(SHIFTS[slot]))
        def _():
            halo_copy(slot).start()

    loads[1].wait()
    loads[2].wait()
    group = lane_group(8, 256)
    delta = jnp.where(group < 4, group - 4, group - 3)
    marks = []
    for w in range(NW):
        for u in (1, -1):
            marks.append(jnp.where(delta == u * offs[w], 1.0, 0.0)[:NB])

    def coef_pair(pair, carry):
        tables = [coup_v[s, pair] for s in range(NS)]
        for atom in range(NA):
            total = jnp.zeros((NB, 256), F32)
            for s in range(NS):
                total = total + jnp.broadcast_to(tables[s][:, atom : atom + 1], (NB, 256)) * marks[s]
            coef[atom, pair, :NB, :] = total
        return carry

    lax.fori_loop(0, 9, coef_pair, 0)

    def make_kernels(atom, carry):
        for slot in range(NB):
            d = []
            for j in range(3):
                block = spread[pl.ds((slot * 3 + j) * NA + atom, NO, stride=ROWS), :]
                derivs[atom, slot * 3 + j] = block.astype(BF16)
                d.append(block)
            for i in range(3):
                for half in range(2):
                    total = None
                    for j in range(3):
                        line = coef[atom, 3 * i + j, slot : slot + 1, half * 128 : (half + 1) * 128]
                        term = jnp.broadcast_to(line, (NO, 128)) * d[j]
                        total = term if total is None else total + term
                    kern[atom, slot, i * NO : (i + 1) * NO, half * 128 : (half + 1) * 128] = total.astype(BF16)
        return carry

    lax.fori_loop(0, NA, make_kernels, 0)

    def place(block, ref, ref_at):
        def chunk_step(chunk, carry):
            for eps in range(2):
                lanes = pl.ds(pl.multiple_of(chunk * 128, 128), 128)
                index = (eps, slice(None), lanes) if ref_at is None else (ref_at, eps, slice(None), lanes)
                tile = ref[index].astype(F32)
                turns = [tile] + [pltpu.roll(tile, NO * k, 1) for k in range(1, 4)]
                for e in range(2):
                    diff = e - (2 * block + eps)
                    if diff == 0 or abs(diff) > 4:
                        continue
                    k = diff + 4 if diff < 0 else diff + 3
                    half, at = k // 4, k % 4
                    for q in range(4):
                        start = pl.multiple_of((chunk * 4 + q) * NA, NA)
                        wide[e * 2 + half, pl.ds(start, NA), at * NO : (at + 1) * NO] = turns[(at - q) % 4][
                            :, at * NO : (at + 1) * NO
                        ]
            return carry

        lax.fori_loop(0, 16, chunk_step, 0)

    loads[3].wait()
    place(0, own, None)
    for slot in (1, 2, 0, 3):
        @pl.when(inside(SHIFTS[slot]))
        def _():
            halo_copy(3 - slot).wait_recv()

        @pl.when(jnp.logical_not(inside(SHIFTS[slot])))
        def _():
            halo[slot] = jnp.zeros(halo.shape[1:], BF16)

        place(SHIFTS[slot], halo, slot)

    def gather_atom(atom, carry):
        for e in range(2):
            for half in range(2):
                part = wide[e * 2 + half, pl.ds(atom, 2 * NO, stride=NA), :]
                blocks[atom, e * 64 : (e + 1) * 64, half * 128 : (half + 1) * 128] = part.astype(BF16)
        return carry

    lax.fori_loop(0, NA, gather_atom, 0)
    loads[4].wait()

    group = lane_group(NO)
    masks = [group == g for g in range(4)]

    def one_atom(atom):
        lefts, rights = [], []
        for slot in range(NB):
            middle = lax.dot_general(
                kern[atom, slot], blocks[near[atom, slot]], NT, preferred_element_type=F32
            ).astype(BF16)
            for i in range(3):
                lefts.append(middle[i * NO : (i + 1) * NO, :])
                block = derivs[atom, slot * 3 + i]
                zero = jnp.zeros_like(block)
                rights.append(jnp.concatenate([jnp.where(mask, block, zero) for mask in masks], axis=0))
        left = jnp.concatenate(lefts, axis=1)
        right = jnp.concatenate(rights, axis=1)
        return lax.dot_general(left, right, NT, preferred_element_type=F32)

    def target(step):
        high = lax.rem(mom // 2 + 1 - step // 2, 2)
        low = lax.rem(mom + (step + 1) // 2, 2)
        return 2 * high + low

    def part_copy(step):
        return pltpu.make_async_remote_copy(
            src_ref=send_buf.at[step],
            dst_ref=recv_buf.at[step],
            send_sem=part_send.at[step],
            recv_sem=part_recv.at[step],
            device_id={"mom": target(step)},
            device_id_type=MESH,
        )

    def part_step(step, carry):
        for at in range(4):
            send_buf[step, at] = one_atom(4 * target(step) + at).astype(BF16)
        part_copy(step).start()
        return carry

    lax.fori_loop(0, 3, part_step, 0)
    for at in range(4):
        sums[at] = one_atom(4 * mom + at)

    for step in range(3):
        part_copy(step).wait_recv()
    for at in range(4):
        total = sums[at]
        for step in range(3):
            total = total + recv_buf[step, at].astype(F32)
        turned[at * 128 : (at + 1) * 128, :] = jnp.concatenate([total] * 4, axis=0).T
    for e in range(2):
        for c in range(2):
            for high in range(8):
                value = None
                for low in range(4):
                    line = turned[pl.ds((e * 2 + c) * 32 + high * 4 + low, 4, stride=128), :]
                    value = line if value is None else jnp.where(masks[low][:4], line, value)
                start = (c * 8 + high) * 128
                out[e, :, start : start + 128] = value

    for slot in range(4):
        @pl.when(inside(SHIFTS[slot]))
        def _():
            halo_copy(slot).wait_send()
    for step in range(3):
        part_copy(step).wait_send()


def body(green, coupling, gradient, neighbours, offsets):
    count, natoms = green.shape[1], green.shape[2]
    anywhere = pl.BlockSpec(memory_space=pl.ANY)
    vmem = pltpu.VMEM
    dma = pltpu.SemaphoreType.DMA
    return pl.pallas_call(
        kernel,
        out_shape=jax.ShapeDtypeStruct((count, natoms // 4, 2 * NO * NO), F32),
        in_specs=[anywhere] * 5,
        out_specs=pl.BlockSpec(memory_space=vmem),
        scratch_shapes=[
            vmem((2, NA, 2048), BF16),
            vmem((4, 2, NA, 2048), BF16),
            vmem((ROWS, 1024), BF16),
            vmem((NS, 9, NB, NA), F32),
            pltpu.SMEM((NA, NB), jnp.int32),
            pltpu.SMEM((NW,), jnp.int32),
            vmem((NO * ROWS, 128), F32),
            vmem((NA, 9, 8, 256), F32),
            vmem((NA, NB, 96, 256), BF16),
            vmem((NA, NB * 3, NO, 128), BF16),
            vmem((4, 64 * NA, 128), F32),
            vmem((NA, 128, 256), BF16),
            vmem((4, NO, 128), F32),
            vmem((3, 4, NO, 128), BF16),
            vmem((3, 4, NO, 128), BF16),
            vmem((512, 128), F32),
            dma((5,)),
            dma((4,)),
            dma((4,)),
            dma((3,)),
            dma((3,)),
        ],
        compiler_params=pltpu.CompilerParams(collective_id=0, has_side_effects=True),
    )(green[0], coupling[0], gradient.reshape(ROWS, NO * NO), neighbours, offsets)


def solution(mesh):
    in_specs = (P("mom", "energy", None, None), P("mom", None, None, None, None), P(), P(), P())
    out_specs = P("energy", "mom", None)
    return jax.shard_map(body, mesh=mesh, in_specs=in_specs, out_specs=out_specs, check_vma=False)
```

time: 159 us -> 31.2 us (0.20); the launches traced: 155 us -> 30.6 us
  matrix products: 53.2 us -> 0 us
  local copies, waits for them, and re-layouts: 55.9 us -> 4.43 us
  Pallas kernels: 0 us -> 26.2 us
  starting transfers between devices: 13.9 us -> 0 us
  blocking collectives: 12.5 us -> 0 us
  loops' own time: 9.8 us -> 0 us
  between operations: 5.93 us -> 0.01 us
  other arithmetic: 4.22 us -> 0 us
    dot_general x10 -> x0, matrix products: 53.2 us -> none  [the longest x5 35.8 us: one_slot(): jnp.einsum('iapm,aiecmn->eacpn', derivs, middle, preferred_element_type=j...]
    pallas_call x0 -> x1, Pallas kernels: none -> 26.2 us  [body(): pl.pallas_call(kernel, out_shape=jax.ShapeDtypeStruct((count, natoms // 4...]
    dynamic_slice x16 -> x0, local copies, waits for them, and re-layouts: 14.3 us -> none  [the longest x5 7.68 us: one_slot(): lax.dynamic_index_in_dim(gradient, slot, 0, keepdims=False)]
    ppermute x4 -> x0, starting transfers between devices: 13.9 us -> none  [shifted_2(): return lax.ppermute(array, axis, pairs)]
    gather x5 -> x0, local copies, waits for them, and re-layouts: 13.2 us -> none  [one_slot(): gathered = jnp.take(blocks, column, axis=2)]
    all_to_all x1 -> x0, blocking collectives: 12.5 us -> none  [sum_at_owner(): lax.all_to_all(split_up(array, dim, length), axis, 0, 0, tiled=True)]
    reshape x10 -> x0, local copies, waits for them, and re-layouts: 9.81 us -> none  [the longest x5 5.97 us: one_slot(): lax.dynamic_index_in_dim(gradient, slot, 0, keepdims=False)]
    another operation x1 -> x0, loops' own time: 9.8 us -> none  [sandwich(): total, _ = lax.scan(one_slot, start_total, jnp.arange(NB, dtype=jnp.int32))]
  transfers between devices with their start and end apart: 4 -> 0, of which waited for: 0 -> 0; matrix products, arithmetic and copies ran while one was open for 3% -> 0% of each run, Pallas kernels for 0% -> 0%
where the time goes in v1:
time: 31.2 us; the launch traced here: 30.6 us
  Pallas kernels  26.2 us (84%)
  local copies, waits for them, and re-layouts  4.43 us (14%)
    pallas_call x1, Pallas kernels, body(): pl.pallas_call(kernel, out_shape=jax.ShapeDtypeStruct((count, natoms // 4...  26.2 us
    unnamed x2, local copies, waits for them, and re-layouts  2.83 us
    squeeze x1, local copies, waits for them, and re-layouts, body(): coupling[0]  1.59 us

profile of v1, /device:TPU:129, one launch (start us, length us, event | category | flops | bytes accessed | tf_op | source)
XLA Modules:
  0.0 30.6 jit_solution(12466295160713962595)
XLA Ops:
  0.0 1.4 %copy.9.neighbours = s32[16,5]{1,0:T(8,128)} copy(s32[16,5]{0,1:T(8,128)} %param.8) | data formatting | bytes 640 | tf_op args[3]
  1.4 1.6 %copy.12 = f32[1,6,9,5,16]{4,3,2,1,0:T(8,128)} copy(f32[1,6,9,5,16]{4,0,3,2,1:T(1,128)} %param.6) | data formatting | bytes 34560 | tf_op jit(solution)/shard_map/squeeze | solution.py:280
  3.0 26.2 %shard_map.55 = f32[2,4,2048]{2,1,0:T(4,128)} custom-call(bf16[2,16,2048]{2,1,0:T(8,128)(2,1)} %bitcast.8, f32[6,9,5,16]{3,2,1,0:T(8,128)} %bitcast.6, bf16[240,1024]{1,0:T(8,128)(2,1)} %bitcast.7, s32[16,5]{1,0:T(8,128)} %copy.9.neighbours, s32[3]{0:T(128)} %offsets.1), custom_call_target="tpu_custom_call" | custom-call | tf_op jit(solution)/shard_map/pallas_call | solution.py:251
  29.2 1.5 %copy.14 = f32[2,4,2048]{2,1,0:T(4,128)} copy(f32[2,4,2048]{2,1,0:T(4,128)} %shard_map.55) | data formatting | bytes 131072

commit v2 on v1

--- a/solution.py
+++ b/solution.py
@@ -101,7 +101,7 @@
             marks.append(jnp.where(delta == u * offs[w], 1.0, 0.0)[:NB])
 
     def coef_pair(pair, carry):
-        tables = [coup_v[s, pair] for s in range(NS)]
+        tables = [coup_v[s, pair, :, 0, :] for s in range(NS)]
         for atom in range(NA):
             total = jnp.zeros((NB, 256), F32)
             for s in range(NS):
@@ -182,7 +182,7 @@
         lefts, rights = [], []
         for slot in range(NB):
             middle = lax.dot_general(
-                kern[atom, slot], blocks[near[atom, slot]], NT, preferred_element_type=F32
+                kern[atom, slot], blocks[near[slot, atom]], NT, preferred_element_type=F32
             ).astype(BF16)
             for i in range(3):
                 lefts.append(middle[i * NO : (i + 1) * NO, :])
@@ -257,8 +257,8 @@
             vmem((2, NA, 2048), BF16),
             vmem((4, 2, NA, 2048), BF16),
             vmem((ROWS, 1024), BF16),
-            vmem((NS, 9, NB, NA), F32),
-            pltpu.SMEM((NA, NB), jnp.int32),
+            vmem((NS, 9, NB, 1, NA), F32),
+            pltpu.SMEM((NB, NA), jnp.int32),
             pltpu.SMEM((NW,), jnp.int32),
             vmem((NO * ROWS, 128), F32),
             vmem((NA, 9, 8, 256), F32),
@@ -277,7 +277,13 @@
             dma((3,)),
         ],
         compiler_params=pltpu.CompilerParams(collective_id=0, has_side_effects=True),
-    )(green[0], coupling[0], gradient.reshape(ROWS, NO * NO), neighbours, offsets)
+    )(
+        green[0],
+        coupling.reshape(NS, 9, NB, 1, NA),
+        gradient.reshape(ROWS, NO * NO),
+        neighbours.T,
+        offsets,
+    )
 
 
 def solution(mesh):

time: 31.2 us -> 30.4 us (0.974)
  the two profiles are of different devices: /device:TPU:129 before, /device:TPU:225 now
where the time goes in v2:
time: 30.4 us; the launch traced here: 30.3 us
  Pallas kernels  28.8 us (95%)
  local copies, waits for them, and re-layouts  1.47 us (5%)
    pallas_call x1, Pallas kernels, body(): pl.pallas_call(kernel, out_shape=jax.ShapeDtypeStruct((count, natoms // 4...  28.8 us
    unnamed x1, local copies, waits for them, and re-layouts  1.47 us

profile of v2, /device:TPU:225, one launch (start us, length us, event | category | flops | bytes accessed | tf_op | source)
XLA Modules:
  0.0 30.3 jit_solution(3590025218759845698)
XLA Ops:
  0.0 28.8 %shard_map.55 = f32[2,4,2048]{2,1,0:T(4,128)} custom-call(bf16[2,16,2048]{2,1,0:T(8,128)(2,1)} %bitcast.6, f32[6,9,5,1,16]{4,3,2,1,0:T(1,128)} %bitcast.5, bf16[240,1024]{1,0:T(8,128)(2,1)} %bitcast.4, s32[5,16]{1,0:T(8,128)} %bitcast.7, s32[3]{0:T(128)} %offsets.1), custom_call_target="tpu_custom_call" | custom-call | tf_op jit(solution)/shard_map/pallas_call | solution.py:251
  28.8 1.5 %copy.7 = f32[2,4,2048]{2,1,0:T(4,128)} copy(f32[2,4,2048]{2,1,0:T(4,128)} %shard_map.55) | data formatting | bytes 131072

commit v3 on v2

--- a/solution.py
+++ b/solution.py
@@ -11,10 +11,11 @@
 NA = 16
 NS = 2 * NW
 ROWS = NB * 3 * NA
+STEP = 68
+GAP = 20
 MESH = pl.DeviceIdType.MESH
 F32 = jnp.float32
 BF16 = jnp.bfloat16
-NT = (((1,), (1,)), ((), ()))
 SHIFTS = (-2, -1, 1, 2)
 
 
@@ -25,7 +26,7 @@
 def kernel(
     green, coupling, gradient, neighbours, offsets, out,
     own, halo, grad_v, coup_v, near, offs,
-    spread, coef, kern, derivs, wide, blocks, sums, send_buf, recv_buf, turned,
+    coup_rows, spread, coef, flipped, kern, derivs, wide, blocks, sums, send_buf, recv_buf, turned,
     local_sem, halo_send, halo_recv, part_send, part_recv,
 ):
     n_energy = lax.axis_size("energy")
@@ -56,22 +57,29 @@
     for by in SHIFTS:
         expected = expected + inside(by).astype(jnp.int32)
 
+    col = lax.broadcasted_iota(jnp.int32, (1, 512), 1)
+    wanted = (col // NO) % 4 * 128 + col // 128 * NO + col % NO
+    rows = lax.broadcasted_iota(jnp.int32, (512, 512), 0)
+    pick = jnp.where(rows == wanted, 1.0, 0.0).astype(BF16)
     loads[0].wait()
-    row = lax.broadcasted_iota(jnp.int32, (128, 512), 0)
-    col = lax.broadcasted_iota(jnp.int32, (128, 512), 1)
-    pick = jnp.where(
-        jnp.logical_and(row // NO == col // 128, row % NO == col % NO), 1.0, 0.0
-    ).astype(BF16)
-
-    def spread_chunk(chunk, carry):
-        part = grad_v[:, pl.ds(pl.multiple_of(chunk * 128, 128), 128)]
-        wide_part = jnp.dot(part, pick, preferred_element_type=F32)
+    lines = []
+    for chunk in range(8):
+        tiles = []
+        for g in range(4):
+            parts = []
+            for tile in range(4):
+                block = 4 * tile + g
+                if block < 3 * NB:
+                    parts.append(grad_v[block * NA : (block + 1) * NA, chunk * 128 : (chunk + 1) * 128])
+                else:
+                    parts.append(jnp.zeros((NA, 128), BF16))
+            tiles.append(jnp.concatenate(parts, axis=0))
+        lines.append(jnp.concatenate(tiles, axis=1))
+    packed = jnp.dot(jnp.concatenate(lines, axis=0), pick, preferred_element_type=F32)
+    for chunk in range(8):
         for q in range(4):
-            start = pl.multiple_of((chunk * 4 + q) * ROWS, 8)
-            spread[pl.ds(start, ROWS), :] = wide_part[:, q * 128 : (q + 1) * 128]
-        return carry
-
-    lax.fori_loop(0, 8, spread_chunk, 0)
+            start = (chunk * 4 + q) * STEP
+            spread[start : start + 64, :] = packed[chunk * 64 : (chunk + 1) * 64, q * 128 : (q + 1) * 128]
 
     pl.semaphore_wait(barrier, expected)
 
@@ -93,39 +101,53 @@
 
     loads[1].wait()
     loads[2].wait()
-    group = lane_group(8, 256)
-    delta = jnp.where(group < 4, group - 4, group - 3)
-    marks = []
-    for w in range(NW):
-        for u in (1, -1):
-            marks.append(jnp.where(delta == u * offs[w], 1.0, 0.0)[:NB])
-
-    def coef_pair(pair, carry):
-        tables = [coup_v[s, pair, :, 0, :] for s in range(NS)]
+
+    def coef_rows(pair, carry):
+        for slot in range(NB):
+            coup_rows[pair, slot : slot + 1, :NA] = coup_v[pair, slot]
+        return carry
+
+    lax.fori_loop(0, NS * 9, coef_rows, 0)
+    group8 = lane_group(8)
+    weights = [
+        [jnp.broadcast_to(jnp.where(offs[w] == size, 1.0, 0.0), (8, 128)) for w in range(NW)] for size in range(1, 5)
+    ]
+
+    def coef_step(j, carry):
+        tables = [[coup_rows[s * 9 + 3 * i + j] for i in range(3)] for s in range(NS)]
         for atom in range(NA):
-            total = jnp.zeros((NB, 256), F32)
+            terms = []
             for s in range(NS):
-                total = total + jnp.broadcast_to(tables[s][:, atom : atom + 1], (NB, 256)) * marks[s]
-            coef[atom, pair, :NB, :] = total
-        return carry
-
-    lax.fori_loop(0, 9, coef_pair, 0)
+                first, second, third = [
+                    jnp.broadcast_to(tables[s][i][:, atom : atom + 1], (8, 128)) for i in range(3)
+                ]
+                terms.append(jnp.where(group8 == 0, first, jnp.where(group8 == 1, second, third)))
+            for size in range(1, 5):
+                for g in range(2):
+                    k = size + 3 if g == 0 else 4 - size
+                    total = None
+                    for w in range(NW):
+                        term = weights[size - 1][w] * terms[2 * w + g]
+                        total = term if total is None else total + term
+                    coef[atom, k * 3 + j] = total
+        return carry
+
+    lax.fori_loop(0, 3, coef_step, 0)
 
     def make_kernels(atom, carry):
+        for tile in range(4):
+            block = spread[pl.ds(tile * NA + atom, NO, stride=STEP), :]
+            derivs[atom, :, tile * 128 : (tile + 1) * 128] = block.astype(BF16)
+            flipped[tile * 128 : (tile + 1) * 128, :] = jnp.concatenate([block] * 4, axis=0).T
         for slot in range(NB):
-            d = []
-            for j in range(3):
-                block = spread[pl.ds((slot * 3 + j) * NA + atom, NO, stride=ROWS), :]
-                derivs[atom, slot * 3 + j] = block.astype(BF16)
-                d.append(block)
-            for i in range(3):
-                for half in range(2):
-                    total = None
-                    for j in range(3):
-                        line = coef[atom, 3 * i + j, slot : slot + 1, half * 128 : (half + 1) * 128]
-                        term = jnp.broadcast_to(line, (NO, 128)) * d[j]
-                        total = term if total is None else total + term
-                    kern[atom, slot, i * NO : (i + 1) * NO, half * 128 : (half + 1) * 128] = total.astype(BF16)
+            d = [flipped[(slot * 3 + j) * NO : (slot * 3 + j + 1) * NO, :] for j in range(3)]
+            for k in range(8):
+                total = None
+                for j in range(3):
+                    line = coef[atom, k * 3 + j, slot : slot + 1, :]
+                    term = jnp.broadcast_to(line, (NO, 128)) * d[j]
+                    total = term if total is None else total + term
+                kern[atom, slot, k * NO : (k + 1) * NO, :] = total.astype(BF16)
         return carry
 
     lax.fori_loop(0, NA, make_kernels, 0)
@@ -144,7 +166,7 @@
                     k = diff + 4 if diff < 0 else diff + 3
                     half, at = k // 4, k % 4
                     for q in range(4):
-                        start = pl.multiple_of((chunk * 4 + q) * NA, NA)
+                        start = pl.multiple_of((chunk * 4 + q) * GAP, 4)
                         wide[e * 2 + half, pl.ds(start, NA), at * NO : (at + 1) * NO] = turns[(at - q) % 4][
                             :, at * NO : (at + 1) * NO
                         ]
@@ -168,7 +190,7 @@
     def gather_atom(atom, carry):
         for e in range(2):
             for half in range(2):
-                part = wide[e * 2 + half, pl.ds(atom, 2 * NO, stride=NA), :]
+                part = wide[e * 2 + half, pl.ds(atom, 2 * NO, stride=GAP), :]
                 blocks[atom, e * 64 : (e + 1) * 64, half * 128 : (half + 1) * 128] = part.astype(BF16)
         return carry
 
@@ -179,19 +201,19 @@
     masks = [group == g for g in range(4)]
 
     def one_atom(atom):
-        lefts, rights = [], []
+        stack = []
         for slot in range(NB):
-            middle = lax.dot_general(
-                kern[atom, slot], blocks[near[slot, atom]], NT, preferred_element_type=F32
-            ).astype(BF16)
+            middle = jnp.dot(blocks[near[slot, atom]], kern[atom, slot], preferred_element_type=F32)
+            parts = [middle[g * NO : (g + 1) * NO, :] for g in range(4)]
             for i in range(3):
-                lefts.append(middle[i * NO : (i + 1) * NO, :])
-                block = derivs[atom, slot * 3 + i]
-                zero = jnp.zeros_like(block)
-                rights.append(jnp.concatenate([jnp.where(mask, block, zero) for mask in masks], axis=0))
-        left = jnp.concatenate(lefts, axis=1)
-        right = jnp.concatenate(rights, axis=1)
-        return lax.dot_general(left, right, NT, preferred_element_type=F32)
+                value = None
+                for g in range(4):
+                    turn = (g - i) % 4
+                    part = pltpu.roll(parts[g], NO * turn, 1) if turn else parts[g]
+                    value = part if value is None else jnp.where(masks[g], part, value)
+                stack.append(value.astype(BF16))
+        stack.append(jnp.zeros((NO, 128), BF16))
+        return jnp.dot(derivs[atom], jnp.concatenate(stack, axis=0), preferred_element_type=F32)
 
     def target(step):
         high = lax.rem(mom // 2 + 1 - step // 2, 2)
@@ -224,16 +246,16 @@
         total = sums[at]
         for step in range(3):
             total = total + recv_buf[step, at].astype(F32)
-        turned[at * 128 : (at + 1) * 128, :] = jnp.concatenate([total] * 4, axis=0).T
-    for e in range(2):
-        for c in range(2):
-            for high in range(8):
-                value = None
-                for low in range(4):
-                    line = turned[pl.ds((e * 2 + c) * 32 + high * 4 + low, 4, stride=128), :]
-                    value = line if value is None else jnp.where(masks[low][:4], line, value)
-                start = (c * 8 + high) * 128
-                out[e, :, start : start + 128] = value
+        for turn in range(4):
+            turned[turn, at * 36 : at * 36 + NO, :] = pltpu.roll(total, NO * turn, 1) if turn else total
+    for g in range(4):
+        for high in range(8):
+            value = None
+            for low in range(4):
+                line = turned[(low - g) % 4, pl.ds(high * 4 + low, 4, stride=36), :]
+                value = line if value is None else jnp.where(masks[low][:4], line, value)
+            start = (g % 2 * 8 + high) * 128
+            out[g // 2, :, start : start + 128] = value
 
     for slot in range(4):
         @pl.when(inside(SHIFTS[slot]))
@@ -257,19 +279,21 @@
             vmem((2, NA, 2048), BF16),
             vmem((4, 2, NA, 2048), BF16),
             vmem((ROWS, 1024), BF16),
-            vmem((NS, 9, NB, 1, NA), F32),
+            vmem((NS * 9, NB, 1, NA), F32),
             pltpu.SMEM((NB, NA), jnp.int32),
             pltpu.SMEM((NW,), jnp.int32),
-            vmem((NO * ROWS, 128), F32),
-            vmem((NA, 9, 8, 256), F32),
-            vmem((NA, NB, 96, 256), BF16),
-            vmem((NA, NB * 3, NO, 128), BF16),
-            vmem((4, 64 * NA, 128), F32),
+            vmem((NS * 9, 8, 128), F32),
+            vmem((NO * STEP, 128), F32),
+            vmem((NA, 24, 8, 128), F32),
+            vmem((512, 128), F32),
+            vmem((NA, NB, 256, 128), BF16),
+            vmem((NA, NO, 512), BF16),
+            vmem((4, 64 * GAP, 128), F32),
             vmem((NA, 128, 256), BF16),
             vmem((4, NO, 128), F32),
             vmem((3, 4, NO, 128), BF16),
             vmem((3, 4, NO, 128), BF16),
-            vmem((512, 128), F32),
+            vmem((4, 4 * 36, 128), F32),
             dma((5,)),
             dma((4,)),
             dma((4,)),
@@ -279,7 +303,7 @@
         compiler_params=pltpu.CompilerParams(collective_id=0, has_side_effects=True),
     )(
         green[0],
-        coupling.reshape(NS, 9, NB, 1, NA),
+        coupling.reshape(NS * 9, NB, 1, NA),
         gradient.reshape(ROWS, NO * NO),
         neighbours.T,
         offsets,

time: 30.4 us -> 26.6 us (0.88)
  the two profiles are of different devices: /device:TPU:225 before, /device:TPU:129 now
where the time goes in v3:
time: 26.6 us; the launch traced here: 26.4 us
  Pallas kernels  24.9 us (94%)
  local copies, waits for them, and re-layouts  1.47 us (6%)
    pallas_call x1, Pallas kernels, body(): pl.pallas_call(kernel, out_shape=jax.ShapeDtypeStruct((count, natoms // 4...  24.9 us
    unnamed x1, local copies, waits for them, and re-layouts  1.47 us

profile of v3, /device:TPU:129, one launch (start us, length us, event | category | flops | bytes accessed | tf_op | source)
XLA Modules:
  0.0 26.4 jit_solution(6757425475335422767)
XLA Ops:
  0.0 24.9 %shard_map.55 = f32[2,4,2048]{2,1,0:T(4,128)} custom-call(bf16[2,16,2048]{2,1,0:T(8,128)(2,1)} %bitcast.6, f32[54,5,1,16]{3,2,1,0:T(1,128)} %bitcast.5, bf16[240,1024]{1,0:T(8,128)(2,1)} %bitcast.4, s32[5,16]{1,0:T(8,128)} %bitcast.7, s32[3]{0:T(128)} %offsets.1), custom_call_target="tpu_custom_call" | custom-call | tf_op jit(solution)/shard_map/pallas_call | solution.py:273
  25.0 1.5 %copy.7 = f32[2,4,2048]{2,1,0:T(4,128)} copy(f32[2,4,2048]{2,1,0:T(4,128)} %shard_map.55) | data formatting | bytes 131072

commit v4 on v3

--- a/solution.py
+++ b/solution.py
@@ -26,7 +26,7 @@
 def kernel(
     green, coupling, gradient, neighbours, offsets, out,
     own, halo, grad_v, coup_v, near, offs,
-    coup_rows, spread, coef, flipped, kern, derivs, wide, blocks, sums, send_buf, recv_buf, turned,
+    coup_rows, spread, coef, flipped, kern, derivs, wide, blocks, send_buf, recv_buf, turned,
     local_sem, halo_send, halo_recv, part_send, part_recv,
 ):
     n_energy = lax.axis_size("energy")
@@ -56,6 +56,24 @@
     expected = 3
     for by in SHIFTS:
         expected = expected + inside(by).astype(jnp.int32)
+
+    pl.semaphore_wait(barrier, expected)
+
+    def halo_copy(slot):
+        by = SHIFTS[slot]
+        return pltpu.make_async_remote_copy(
+            src_ref=green,
+            dst_ref=halo.at[3 - slot],
+            send_sem=halo_send.at[slot],
+            recv_sem=halo_recv.at[3 - slot],
+            device_id={"energy": energy + by},
+            device_id_type=MESH,
+        )
+
+    for slot in range(4):
+        @pl.when(inside(SHIFTS[slot]))
+        def _():
+            halo_copy(slot).start()
 
     col = lax.broadcasted_iota(jnp.int32, (1, 512), 1)
     wanted = (col // NO) % 4 * 128 + col // 128 * NO + col % NO
@@ -81,33 +99,12 @@
             start = (chunk * 4 + q) * STEP
             spread[start : start + 64, :] = packed[chunk * 64 : (chunk + 1) * 64, q * 128 : (q + 1) * 128]
 
-    pl.semaphore_wait(barrier, expected)
-
-    def halo_copy(slot):
-        by = SHIFTS[slot]
-        return pltpu.make_async_remote_copy(
-            src_ref=green,
-            dst_ref=halo.at[3 - slot],
-            send_sem=halo_send.at[slot],
-            recv_sem=halo_recv.at[3 - slot],
-            device_id={"energy": energy + by},
-            device_id_type=MESH,
-        )
-
-    for slot in range(4):
-        @pl.when(inside(SHIFTS[slot]))
-        def _():
-            halo_copy(slot).start()
-
     loads[1].wait()
     loads[2].wait()
 
-    def coef_rows(pair, carry):
+    for pair in range(NS * 9):
         for slot in range(NB):
             coup_rows[pair, slot : slot + 1, :NA] = coup_v[pair, slot]
-        return carry
-
-    lax.fori_loop(0, NS * 9, coef_rows, 0)
     group8 = lane_group(8)
     weights = [
         [jnp.broadcast_to(jnp.where(offs[w] == size, 1.0, 0.0), (8, 128)) for w in range(NW)] for size in range(1, 5)
@@ -124,7 +121,7 @@
                 terms.append(jnp.where(group8 == 0, first, jnp.where(group8 == 1, second, third)))
             for size in range(1, 5):
                 for g in range(2):
-                    k = size + 3 if g == 0 else 4 - size
+                    k = 4 * g + size - 1
                     total = None
                     for w in range(NW):
                         term = weights[size - 1][w] * terms[2 * w + g]
@@ -152,31 +149,36 @@
 
     lax.fori_loop(0, NA, make_kernels, 0)
 
-    def place(block, ref, ref_at):
+    group16 = lane_group(NA)
+
+    def place(block, load):
         def chunk_step(chunk, carry):
+            turns = []
             for eps in range(2):
-                lanes = pl.ds(pl.multiple_of(chunk * 128, 128), 128)
-                index = (eps, slice(None), lanes) if ref_at is None else (ref_at, eps, slice(None), lanes)
-                tile = ref[index].astype(F32)
-                turns = [tile] + [pltpu.roll(tile, NO * k, 1) for k in range(1, 4)]
-                for e in range(2):
-                    diff = e - (2 * block + eps)
-                    if diff == 0 or abs(diff) > 4:
+                tile = load(eps, pl.ds(pl.multiple_of(chunk * 128, 128), 128)).astype(F32)
+                turns.append([tile] + [pltpu.roll(tile, NO * k, 1) for k in range(1, 4)])
+            for e in range(2):
+                for half in range(2):
+                    found = {}
+                    for eps in range(2):
+                        diff = (e - (2 * block + eps)) * (1 - 2 * half)
+                        if 1 <= diff <= 4:
+                            found[diff - 1] = eps
+                    if not found:
                         continue
-                    k = diff + 4 if diff < 0 else diff + 3
-                    half, at = k // 4, k % 4
+                    low, high = min(found), max(found)
                     for q in range(4):
+                        value = turns[found[low]][(low - q) % 4]
+                        if high > low:
+                            value = jnp.where(group16 == low, value, turns[found[high]][(high - q) % 4])
                         start = pl.multiple_of((chunk * 4 + q) * GAP, 4)
-                        wide[e * 2 + half, pl.ds(start, NA), at * NO : (at + 1) * NO] = turns[(at - q) % 4][
-                            :, at * NO : (at + 1) * NO
-                        ]
+                        lanes = slice(low * NO, (high + 1) * NO)
+                        wide[e * 2 + half, pl.ds(start, NA), lanes] = value[:, lanes]
             return carry
 
         lax.fori_loop(0, 16, chunk_step, 0)
 
-    loads[3].wait()
-    place(0, own, None)
-    for slot in (1, 2, 0, 3):
+    def receive(slot):
         @pl.when(inside(SHIFTS[slot]))
         def _():
             halo_copy(3 - slot).wait_recv()
@@ -185,25 +187,34 @@
         def _():
             halo[slot] = jnp.zeros(halo.shape[1:], BF16)
 
-        place(SHIFTS[slot], halo, slot)
-
-    def gather_atom(atom, carry):
-        for e in range(2):
-            for half in range(2):
+        place(SHIFTS[slot], lambda eps, lanes: halo[slot, eps, :, lanes])
+
+    def gather(half):
+        def gather_atom(atom, carry):
+            for e in range(2):
                 part = wide[e * 2 + half, pl.ds(atom, 2 * NO, stride=GAP), :]
                 blocks[atom, e * 64 : (e + 1) * 64, half * 128 : (half + 1) * 128] = part.astype(BF16)
-        return carry
-
-    lax.fori_loop(0, NA, gather_atom, 0)
+            return carry
+
+        lax.fori_loop(0, NA, gather_atom, 0)
+
+    loads[3].wait()
+    place(0, lambda eps, lanes: own[eps, :, lanes])
+    receive(0)
+    receive(3)
+    receive(1)
+    gather(0)
+    receive(2)
+    gather(1)
     loads[4].wait()
 
     group = lane_group(NO)
     masks = [group == g for g in range(4)]
 
-    def one_atom(atom):
+    def first_step(atom):
         stack = []
         for slot in range(NB):
-            middle = jnp.dot(blocks[near[slot, atom]], kern[atom, slot], preferred_element_type=F32)
+            middle = jnp.dot(blocks[near[slot, atom]], kern[atom, slot], preferred_element_type=F32).astype(BF16)
             parts = [middle[g * NO : (g + 1) * NO, :] for g in range(4)]
             for i in range(3):
                 value = None
@@ -211,9 +222,22 @@
                     turn = (g - i) % 4
                     part = pltpu.roll(parts[g], NO * turn, 1) if turn else parts[g]
                     value = part if value is None else jnp.where(masks[g], part, value)
-                stack.append(value.astype(BF16))
+                stack.append(value)
         stack.append(jnp.zeros((NO, 128), BF16))
-        return jnp.dot(derivs[atom], jnp.concatenate(stack, axis=0), preferred_element_type=F32)
+        return jnp.concatenate(stack, axis=0)
+
+    def second_step(atom, stack):
+        return jnp.dot(derivs[atom], stack, preferred_element_type=F32)
+
+    def four_atoms(group):
+        atoms = [4 * group + at for at in range(4)]
+        stacks, results = [], []
+        for at in range(4):
+            stacks.append(first_step(atoms[at]))
+            if at:
+                results.append(second_step(atoms[at - 1], stacks[at - 1]))
+        results.append(second_step(atoms[3], stacks[3]))
+        return results
 
     def target(step):
         high = lax.rem(mom // 2 + 1 - step // 2, 2)
@@ -231,19 +255,18 @@
         )
 
     def part_step(step, carry):
-        for at in range(4):
-            send_buf[step, at] = one_atom(4 * target(step) + at).astype(BF16)
+        for at, part in enumerate(four_atoms(target(step))):
+            send_buf[step, at] = part.astype(BF16)
         part_copy(step).start()
         return carry
 
     lax.fori_loop(0, 3, part_step, 0)
-    for at in range(4):
-        sums[at] = one_atom(4 * mom + at)
+    own_parts = four_atoms(mom)
 
     for step in range(3):
         part_copy(step).wait_recv()
     for at in range(4):
-        total = sums[at]
+        total = own_parts[at]
         for step in range(3):
             total = total + recv_buf[step, at].astype(F32)
         for turn in range(4):
@@ -290,7 +313,6 @@
             vmem((NA, NO, 512), BF16),
             vmem((4, 64 * GAP, 128), F32),
             vmem((NA, 128, 256), BF16),
-            vmem((4, NO, 128), F32),
             vmem((3, 4, NO, 128), BF16),
             vmem((3, 4, NO, 128), BF16),
             vmem((4, 4 * 36, 128), F32),

time: 26.6 us -> 26 us (0.977)
  the two profiles are of different devices: /device:TPU:129 before, /device:TPU:137 now
where the time goes in v4:
time: 26 us; the launch traced here: 25.9 us
  Pallas kernels  24.4 us (94%)
  local copies, waits for them, and re-layouts  1.47 us (6%)
    pallas_call x1, Pallas kernels, body(): pl.pallas_call(kernel, out_shape=jax.ShapeDtypeStruct((count, natoms // 4...  24.4 us
    unnamed x1, local copies, waits for them, and re-layouts  1.47 us

profile of v4, /device:TPU:137, one launch (start us, length us, event | category | flops | bytes accessed | tf_op | source)
XLA Modules:
  0.0 25.9 jit_solution(10681973378573103650)
XLA Ops:
  0.0 24.4 %shard_map.55 = f32[2,4,2048]{2,1,0:T(4,128)} custom-call(bf16[2,16,2048]{2,1,0:T(8,128)(2,1)} %bitcast.6, f32[54,5,1,16]{3,2,1,0:T(1,128)} %bitcast.5, bf16[240,1024]{1,0:T(8,128)(2,1)} %bitcast.4, s32[5,16]{1,0:T(8,128)} %bitcast.7, s32[3]{0:T(128)} %offsets.1), custom_call_target="tpu_custom_call" | custom-call | tf_op jit(solution)/shard_map/pallas_call | solution.py:296
  24.4 1.5 %copy.7 = f32[2,4,2048]{2,1,0:T(4,128)} copy(f32[2,4,2048]{2,1,0:T(4,128)} %shard_map.55) | data formatting | bytes 131072

commit v5 on v4

--- a/solution.py
+++ b/solution.py
@@ -70,7 +70,7 @@
             device_id_type=MESH,
         )
 
-    for slot in range(4):
+    for slot in (0, 3, 1, 2):
         @pl.when(inside(SHIFTS[slot]))
         def _():
             halo_copy(slot).start()
@@ -151,45 +151,41 @@
 
     group16 = lane_group(NA)
 
-    def place(block, load):
+    masks16 = [group16 == g for g in range(4)]
+
+    def arrive(slot):
+        @pl.when(inside(SHIFTS[slot]))
+        def _():
+            halo_copy(3 - slot).wait_recv()
+
+        @pl.when(jnp.logical_not(inside(SHIFTS[slot])))
+        def _():
+            halo[slot] = jnp.zeros(halo.shape[1:], BF16)
+
+    def place(half):
         def chunk_step(chunk, carry):
-            turns = []
-            for eps in range(2):
-                tile = load(eps, pl.ds(pl.multiple_of(chunk * 128, 128), 128)).astype(F32)
-                turns.append([tile] + [pltpu.roll(tile, NO * k, 1) for k in range(1, 4)])
+            lanes = pl.ds(pl.multiple_of(chunk * 128, 128), 128)
+            turns = {}
             for e in range(2):
-                for half in range(2):
-                    found = {}
-                    for eps in range(2):
-                        diff = (e - (2 * block + eps)) * (1 - 2 * half)
-                        if 1 <= diff <= 4:
-                            found[diff - 1] = eps
-                    if not found:
-                        continue
-                    low, high = min(found), max(found)
-                    for q in range(4):
-                        value = turns[found[low]][(low - q) % 4]
-                        if high > low:
-                            value = jnp.where(group16 == low, value, turns[found[high]][(high - q) % 4])
-                        start = pl.multiple_of((chunk * 4 + q) * GAP, 4)
-                        lanes = slice(low * NO, (high + 1) * NO)
-                        wide[e * 2 + half, pl.ds(start, NA), lanes] = value[:, lanes]
+                for at in range(4):
+                    row = e - (at + 1) * (1 - 2 * half)
+                    if row not in turns:
+                        block, eps = row // 2, row % 2
+                        tile = own[eps, :, lanes] if block == 0 else halo[SHIFTS.index(block), eps, :, lanes]
+                        tile = tile.astype(F32)
+                        turns[row] = [tile] + [pltpu.roll(tile, NO * k, 1) for k in range(1, 4)]
+            for e in range(2):
+                for q in range(4):
+                    value = None
+                    for at in range(4):
+                        part = turns[e - (at + 1) * (1 - 2 * half)][(at - q) % 4]
+                        value = part if value is None else jnp.where(masks16[at], part, value)
+                    start = pl.multiple_of((chunk * 4 + q) * GAP, 4)
+                    wide[e * 2 + half, pl.ds(start, NA), :] = value
             return carry
 
         lax.fori_loop(0, 16, chunk_step, 0)
 
-    def receive(slot):
-        @pl.when(inside(SHIFTS[slot]))
-        def _():
-            halo_copy(3 - slot).wait_recv()
-
-        @pl.when(jnp.logical_not(inside(SHIFTS[slot])))
-        def _():
-            halo[slot] = jnp.zeros(halo.shape[1:], BF16)
-
-        place(SHIFTS[slot], lambda eps, lanes: halo[slot, eps, :, lanes])
-
-    def gather(half):
         def gather_atom(atom, carry):
             for e in range(2):
                 part = wide[e * 2 + half, pl.ds(atom, 2 * NO, stride=GAP), :]
@@ -199,13 +195,24 @@
         lax.fori_loop(0, NA, gather_atom, 0)
 
     loads[3].wait()
-    place(0, lambda eps, lanes: own[eps, :, lanes])
-    receive(0)
-    receive(3)
-    receive(1)
-    gather(0)
-    receive(2)
-    gather(1)
+    arrive(0)
+    arrive(3)
+    even = lax.rem(energy, 2) == 0
+
+    @pl.when(even)
+    def _():
+        arrive(2)
+        place(1)
+        arrive(1)
+        place(0)
+
+    @pl.when(jnp.logical_not(even))
+    def _():
+        arrive(1)
+        place(0)
+        arrive(2)
+        place(1)
+
     loads[4].wait()
 
     group = lane_group(NO)
@@ -295,7 +302,7 @@
     dma = pltpu.SemaphoreType.DMA
     return pl.pallas_call(
         kernel,
-        out_shape=jax.ShapeDtypeStruct((count, natoms // 4, 2 * NO * NO), F32),
+        out_shape=pltpu.VMEM((count, natoms // 4, 2 * NO * NO), F32),
         in_specs=[anywhere] * 5,
         out_specs=pl.BlockSpec(memory_space=vmem),
         scratch_shapes=[

time: 26 us -> 22.3 us (0.86)
  the two profiles are of different devices: /device:TPU:137 before, /device:TPU:129 now
where the time goes in v5:
time: 22.3 us; the launch traced here: 22.2 us
  Pallas kernels  21.6 us (97%)
  local copies, waits for them, and re-layouts  0.63 us (3%)
    pallas_call x1, Pallas kernels, body(): pl.pallas_call(kernel, out_shape=pltpu.VMEM((count, natoms // 4, 2 * NO *...  21.6 us
    unnamed x1, local copies, waits for them, and re-layouts  0.63 us

profile of v5, /device:TPU:129, one launch (start us, length us, event | category | flops | bytes accessed | tf_op | source)
XLA Modules:
  0.0 22.2 jit_solution(12540512962888526019)
XLA Ops:
  0.0 21.6 %shard_map.55 = f32[2,4,2048]{2,1,0:T(4,128)S(1)} custom-call(bf16[2,16,2048]{2,1,0:T(8,128)(2,1)} %bitcast.6, f32[54,5,1,16]{3,2,1,0:T(1,128)} %bitcast.5, bf16[240,1024]{1,0:T(8,128)(2,1)} %bitcast.4, s32[5,16]{1,0:T(8,128)} %bitcast.7, s32[3]{0:T(128)} %offsets.1), custom_call_target="tpu_custom_call" | custom-call | tf_op jit(solution)/shard_map/pallas_call | solution.py:303
  21.6 0.6 %copy.7 = f32[2,4,2048]{2,1,0:T(4,128)} copy(f32[2,4,2048]{2,1,0:T(4,128)S(1)} %shard_map.55) | data formatting | bytes 131072

commit v6 on v5

--- a/solution.py
+++ b/solution.py
@@ -172,7 +172,6 @@
                     if row not in turns:
                         block, eps = row // 2, row % 2
                         tile = own[eps, :, lanes] if block == 0 else halo[SHIFTS.index(block), eps, :, lanes]
-                        tile = tile.astype(F32)
                         turns[row] = [tile] + [pltpu.roll(tile, NO * k, 1) for k in range(1, 4)]
             for e in range(2):
                 for q in range(4):
@@ -181,10 +180,10 @@
                         part = turns[e - (at + 1) * (1 - 2 * half)][(at - q) % 4]
                         value = part if value is None else jnp.where(masks16[at], part, value)
                     start = pl.multiple_of((chunk * 4 + q) * GAP, 4)
-                    wide[e * 2 + half, pl.ds(start, NA), :] = value
+                    wide[e * 2 + half, pl.ds(start, NA), :] = value.astype(F32)
             return carry
 
-        lax.fori_loop(0, 16, chunk_step, 0)
+        lax.fori_loop(0, 16, chunk_step, 0, unroll=4)
 
         def gather_atom(atom, carry):
             for e in range(2):
@@ -192,7 +191,7 @@
                 blocks[atom, e * 64 : (e + 1) * 64, half * 128 : (half + 1) * 128] = part.astype(BF16)
             return carry
 
-        lax.fori_loop(0, NA, gather_atom, 0)
+        lax.fori_loop(0, NA, gather_atom, 0, unroll=4)
 
     loads[3].wait()
     arrive(0)

time: 22.3 us -> 21.4 us (0.960)
  Pallas kernels: 21.6 us -> 20.6 us
    pallas_call x1, Pallas kernels: 21.6 us -> 20.6 us  [body(): pl.pallas_call(kernel, out_shape=pltpu.VMEM((count, natoms // 4, 2 * NO *...]
where the time goes in v6:
time: 21.4 us; the launch traced here: 21.3 us
  Pallas kernels  20.6 us (96%)
  local copies, waits for them, and re-layouts  0.63 us (3%)
    pallas_call x1, Pallas kernels, body(): pl.pallas_call(kernel, out_shape=pltpu.VMEM((count, natoms // 4, 2 * NO *...  20.6 us
    unnamed x1, local copies, waits for them, and re-layouts  0.63 us

profile of v6, /device:TPU:129, one launch (start us, length us, event | category | flops | bytes accessed | tf_op | source)
XLA Modules:
  0.0 21.3 jit_solution(1468438447838644375)
XLA Ops:
  0.0 20.6 %shard_map.55 = f32[2,4,2048]{2,1,0:T(4,128)S(1)} custom-call(bf16[2,16,2048]{2,1,0:T(8,128)(2,1)} %bitcast.6, f32[54,5,1,16]{3,2,1,0:T(1,128)} %bitcast.5, bf16[240,1024]{1,0:T(8,128)(2,1)} %bitcast.4, s32[5,16]{1,0:T(8,128)} %bitcast.7, s32[3]{0:T(128)} %offsets.1), custom_call_target="tpu_custom_call" | custom-call | tf_op jit(solution)/shard_map/pallas_call | solution.py:302
  20.7 0.6 %copy.7 = f32[2,4,2048]{2,1,0:T(4,128)} copy(f32[2,4,2048]{2,1,0:T(4,128)S(1)} %shard_map.55) | data formatting | bytes 131072

commit v7 on v6

--- a/solution.py
+++ b/solution.py
@@ -235,16 +235,6 @@
     def second_step(atom, stack):
         return jnp.dot(derivs[atom], stack, preferred_element_type=F32)
 
-    def four_atoms(group):
-        atoms = [4 * group + at for at in range(4)]
-        stacks, results = [], []
-        for at in range(4):
-            stacks.append(first_step(atoms[at]))
-            if at:
-                results.append(second_step(atoms[at - 1], stacks[at - 1]))
-        results.append(second_step(atoms[3], stacks[3]))
-        return results
-
     def target(step):
         high = lax.rem(mom // 2 + 1 - step // 2, 2)
         low = lax.rem(mom + (step + 1) // 2, 2)
@@ -260,14 +250,26 @@
             device_id_type=MESH,
         )
 
-    def part_step(step, carry):
-        for at, part in enumerate(four_atoms(target(step))):
-            send_buf[step, at] = part.astype(BF16)
-        part_copy(step).start()
-        return carry
-
-    lax.fori_loop(0, 3, part_step, 0)
-    own_parts = four_atoms(mom)
+    own_parts = []
+
+    def finish(step, at, atom, stack):
+        part = second_step(atom, stack)
+        if step == 3:
+            own_parts.append(part)
+            return
+        send_buf[step, at] = part.astype(BF16)
+        if at == 3:
+            part_copy(step).start()
+
+    waiting = None
+    for step in range(4):
+        for at in range(4):
+            atom = 4 * target(step) + at
+            stack = first_step(atom)
+            if waiting is not None:
+                finish(*waiting)
+            waiting = (step, at, atom, stack)
+    finish(*waiting)
 
     for step in range(3):
         part_copy(step).wait_recv()

time: 21.4 us -> 21.2 us (level)
  no operation moved by 1% of the time
where the time goes in v7:
time: 21.2 us; the launch traced here: 21.1 us
  Pallas kernels  20.5 us (97%)
  local copies, waits for them, and re-layouts  0.63 us (3%)
    pallas_call x1, Pallas kernels, body(): pl.pallas_call(kernel, out_shape=pltpu.VMEM((count, natoms // 4, 2 * NO *...  20.5 us
    unnamed x1, local copies, waits for them, and re-layouts  0.63 us

profile of v7, /device:TPU:129, one launch (start us, length us, event | category | flops | bytes accessed | tf_op | source)
XLA Modules:
  0.0 21.1 jit_solution(14030366105913476349)
XLA Ops:
  0.0 20.5 %shard_map.55 = f32[2,4,2048]{2,1,0:T(4,128)S(1)} custom-call(bf16[2,16,2048]{2,1,0:T(8,128)(2,1)} %bitcast.6, f32[54,5,1,16]{3,2,1,0:T(1,128)} %bitcast.5, bf16[240,1024]{1,0:T(8,128)(2,1)} %bitcast.4, s32[5,16]{1,0:T(8,128)} %bitcast.7, s32[3]{0:T(128)} %offsets.1), custom_call_target="tpu_custom_call" | custom-call | tf_op jit(solution)/shard_map/pallas_call | solution.py:304
  20.5 0.6 %copy.7 = f32[2,4,2048]{2,1,0:T(4,128)} copy(f32[2,4,2048]{2,1,0:T(4,128)S(1)} %shard_map.55) | data formatting | bytes 131072

commit v8 on v7

--- a/solution.py
+++ b/solution.py
@@ -13,6 +13,7 @@
 ROWS = NB * 3 * NA
 STEP = 68
 GAP = 20
+STOPS = (0, 0, 2, 3)
 MESH = pl.DeviceIdType.MESH
 F32 = jnp.float32
 BF16 = jnp.bfloat16
@@ -47,33 +48,61 @@
         return jnp.logical_and(energy + by >= 0, energy + by < n_energy)
 
     barrier = pltpu.get_barrier_semaphore()
-    for by in SHIFTS:
+    odd = lax.rem(energy, 2)
+    mate = energy + 1 - 2 * odd
+    for by in (-2, 2):
         @pl.when(inside(by))
         def _():
             pl.semaphore_signal(barrier, inc=1, device_id={"energy": energy + by}, device_id_type=MESH)
+    pl.semaphore_signal(barrier, inc=1, device_id={"energy": mate}, device_id_type=MESH)
     for step in range(1, 4):
         pl.semaphore_signal(barrier, inc=1, device_id={"mom": lax.rem(mom + step, 4)}, device_id_type=MESH)
-    expected = 3
-    for by in SHIFTS:
+    expected = 4
+    for by in (-2, 2):
         expected = expected + inside(by).astype(jnp.int32)
 
     pl.semaphore_wait(barrier, expected)
 
-    def halo_copy(slot):
-        by = SHIFTS[slot]
+    def halo_copy(source, eps, slot, kind, peer):
         return pltpu.make_async_remote_copy(
-            src_ref=green,
-            dst_ref=halo.at[3 - slot],
-            send_sem=halo_send.at[slot],
-            recv_sem=halo_recv.at[3 - slot],
-            device_id={"energy": energy + by},
+            src_ref=source.at[eps // 2, :, eps % 2 * 1024 : eps % 2 * 1024 + 1024],
+            dst_ref=halo.at[slot, eps // 2, :, eps % 2 * 1024 : eps % 2 * 1024 + 1024],
+            send_sem=halo_send.at[kind, eps],
+            recv_sem=halo_recv.at[slot, eps],
+            device_id={"energy": peer},
             device_id_type=MESH,
         )
 
-    for slot in (0, 3, 1, 2):
-        @pl.when(inside(SHIFTS[slot]))
-        def _():
-            halo_copy(slot).start()
+    def up(eps):
+        return halo_copy(green, eps, 0, 0, energy + 2)
+
+    def down(eps):
+        return halo_copy(green, eps, 3, 1, energy - 2)
+
+    def across_pair(eps):
+        return halo_copy(green, eps, 1 + odd, 2, mate)
+
+    def forward(eps):
+        return halo_copy(halo.at[3 - 3 * odd], eps, 2 - odd, 3, mate)
+
+    def arrived(slot, eps):
+        halo_copy(green, eps, slot, 0, mate).wait_recv()
+
+    passing = jnp.logical_or(jnp.logical_and(odd == 0, inside(2)), jnp.logical_and(odd == 1, inside(-2)))
+    for eps in range(4):
+        @pl.when(inside(-2))
+        def _():
+            down(eps).start()
+
+        @pl.when(inside(2))
+        def _():
+            up(eps).start()
+
+        across_pair(eps).start()
+    for slot in range(4):
+        @pl.when(jnp.logical_not(inside(SHIFTS[slot])))
+        def _():
+            halo[slot] = jnp.zeros(halo.shape[1:], BF16)
 
     col = lax.broadcasted_iota(jnp.int32, (1, 512), 1)
     wanted = (col // NO) % 4 * 128 + col // 128 * NO + col % NO
@@ -147,7 +176,19 @@
                 kern[atom, slot, k * NO : (k + 1) * NO, :] = total.astype(BF16)
         return carry
 
-    lax.fori_loop(0, NA, make_kernels, 0)
+    def pass_on(eps):
+        @pl.when(passing)
+        def _():
+            arrived(3 - 3 * odd, eps)
+            forward(eps).start()
+
+    done = 0
+    for eps, stop in enumerate(STOPS):
+        if stop > done:
+            lax.fori_loop(done, stop, make_kernels, 0)
+        done = stop
+        pass_on(eps)
+    lax.fori_loop(done, NA, make_kernels, 0)
 
     group16 = lane_group(NA)
 
@@ -156,11 +197,8 @@
     def arrive(slot):
         @pl.when(inside(SHIFTS[slot]))
         def _():
-            halo_copy(3 - slot).wait_recv()
-
-        @pl.when(jnp.logical_not(inside(SHIFTS[slot])))
-        def _():
-            halo[slot] = jnp.zeros(halo.shape[1:], BF16)
+            for eps in range(4):
+                arrived(slot, eps)
 
     def place(half):
         def chunk_step(chunk, carry):
@@ -194,21 +232,19 @@
         lax.fori_loop(0, NA, gather_atom, 0, unroll=4)
 
     loads[3].wait()
-    arrive(0)
-    arrive(3)
-    even = lax.rem(energy, 2) == 0
-
-    @pl.when(even)
+    @pl.when(odd == 0)
     def _():
         arrive(2)
         place(1)
+        arrive(0)
         arrive(1)
         place(0)
 
-    @pl.when(jnp.logical_not(even))
+    @pl.when(odd == 1)
     def _():
         arrive(1)
         place(0)
+        arrive(3)
         arrive(2)
         place(1)
 
@@ -271,12 +307,12 @@
             waiting = (step, at, atom, stack)
     finish(*waiting)
 
-    for step in range(3):
-        part_copy(step).wait_recv()
+    part_copy(2).wait_recv()
+    sums = [own_parts[at] + recv_buf[2, at].astype(F32) for at in range(4)]
+    part_copy(0).wait_recv()
+    part_copy(1).wait_recv()
     for at in range(4):
-        total = own_parts[at]
-        for step in range(3):
-            total = total + recv_buf[step, at].astype(F32)
+        total = sums[at] + recv_buf[0, at].astype(F32) + recv_buf[1, at].astype(F32)
         for turn in range(4):
             turned[turn, at * 36 : at * 36 + NO, :] = pltpu.roll(total, NO * turn, 1) if turn else total
     for g in range(4):
@@ -288,10 +324,21 @@
             start = (g % 2 * 8 + high) * 128
             out[g // 2, :, start : start + 128] = value
 
-    for slot in range(4):
-        @pl.when(inside(SHIFTS[slot]))
-        def _():
-            halo_copy(slot).wait_send()
+    for eps in range(4):
+        @pl.when(inside(-2))
+        def _():
+            down(eps).wait_send()
+
+        @pl.when(inside(2))
+        def _():
+            up(eps).wait_send()
+
+        across_pair(eps).wait_send()
+
+        @pl.when(passing)
+        def _():
+            forward(eps).wait_send()
+
     for step in range(3):
         part_copy(step).wait_send()
 
@@ -325,8 +372,8 @@
             vmem((3, 4, NO, 128), BF16),
             vmem((4, 4 * 36, 128), F32),
             dma((5,)),
-            dma((4,)),
-            dma((4,)),
+            dma((4, 4)),
+            dma((4, 4)),
             dma((3,)),
             dma((3,)),
         ],

time: 21.2 us -> 20.8 us (0.981)
  Pallas kernels: 20.5 us -> 20 us
    pallas_call x1, Pallas kernels: 20.5 us -> 20 us  [body(): pl.pallas_call(kernel, out_shape=pltpu.VMEM((count, natoms // 4, 2 * NO *...]
where the time goes in v8:
time: 20.8 us; the launch traced here: 20.7 us
  Pallas kernels  20 us (96%)
  local copies, waits for them, and re-layouts  0.63 us (3%)
    pallas_call x1, Pallas kernels, body(): pl.pallas_call(kernel, out_shape=pltpu.VMEM((count, natoms // 4, 2 * NO *...  20 us
    unnamed x1, local copies, waits for them, and re-layouts  0.63 us

profile of v8, /device:TPU:129, one launch (start us, length us, event | category | flops | bytes accessed | tf_op | source)
XLA Modules:
  0.0 20.7 jit_solution(3060013802395945991)
XLA Ops:
  0.0 20.0 %shard_map.55 = f32[2,4,2048]{2,1,0:T(4,128)S(1)} custom-call(bf16[2,16,2048]{2,1,0:T(8,128)(2,1)} %bitcast.6, f32[54,5,1,16]{3,2,1,0:T(1,128)} %bitcast.5, bf16[240,1024]{1,0:T(8,128)(2,1)} %bitcast.4, s32[5,16]{1,0:T(8,128)} %bitcast.7, s32[3]{0:T(128)} %offsets.1), custom_call_target="tpu_custom_call" | custom-call | tf_op jit(solution)/shard_map/pallas_call | solution.py:351
  20.1 0.6 %copy.7 = f32[2,4,2048]{2,1,0:T(4,128)} copy(f32[2,4,2048]{2,1,0:T(4,128)S(1)} %shard_map.55) | data formatting | bytes 131072

commit v9 on v8

--- a/solution.py
+++ b/solution.py
@@ -41,8 +41,6 @@
         pltpu.make_async_copy(green, own, local_sem.at[3]),
         pltpu.make_async_copy(neighbours, near, local_sem.at[4]),
     ]
-    for load in loads:
-        load.start()
 
     def inside(by):
         return jnp.logical_and(energy + by >= 0, energy + by < n_energy)
@@ -57,6 +55,8 @@
     pl.semaphore_signal(barrier, inc=1, device_id={"energy": mate}, device_id_type=MESH)
     for step in range(1, 4):
         pl.semaphore_signal(barrier, inc=1, device_id={"mom": lax.rem(mom + step, 4)}, device_id_type=MESH)
+    for load in loads:
+        load.start()
     expected = 4
     for by in (-2, 2):
         expected = expected + inside(by).astype(jnp.int32)
@@ -221,7 +221,7 @@
                     wide[e * 2 + half, pl.ds(start, NA), :] = value.astype(F32)
             return carry
 
-        lax.fori_loop(0, 16, chunk_step, 0, unroll=4)
+        lax.fori_loop(0, 16, chunk_step, 0, unroll=8)
 
         def gather_atom(atom, carry):
             for e in range(2):
@@ -229,7 +229,7 @@
                 blocks[atom, e * 64 : (e + 1) * 64, half * 128 : (half + 1) * 128] = part.astype(BF16)
             return carry
 
-        lax.fori_loop(0, NA, gather_atom, 0, unroll=4)
+        lax.fori_loop(0, NA, gather_atom, 0, unroll=8)
 
     loads[3].wait()
     @pl.when(odd == 0)

time: 20.8 us -> 20.6 us (level)
  no operation moved by 1% of the time
where the time goes in v9:
time: 20.6 us; the launch traced here: 20.5 us
  Pallas kernels  19.9 us (97%)
  local copies, waits for them, and re-layouts  0.63 us (3%)
    pallas_call x1, Pallas kernels, body(): pl.pallas_call(kernel, out_shape=pltpu.VMEM((count, natoms // 4, 2 * NO *...  19.9 us
    unnamed x1, local copies, waits for them, and re-layouts  0.63 us

profile of v9, /device:TPU:129, one launch (start us, length us, event | category | flops | bytes accessed | tf_op | source)
XLA Modules:
  0.0 20.5 jit_solution(14951660658460882561)
XLA Ops:
  0.0 19.9 %shard_map.55 = f32[2,4,2048]{2,1,0:T(4,128)S(1)} custom-call(bf16[2,16,2048]{2,1,0:T(8,128)(2,1)} %bitcast.6, f32[54,5,1,16]{3,2,1,0:T(1,128)} %bitcast.5, bf16[240,1024]{1,0:T(8,128)(2,1)} %bitcast.4, s32[5,16]{1,0:T(8,128)} %bitcast.7, s32[3]{0:T(128)} %offsets.1), custom_call_target="tpu_custom_call" | custom-call | tf_op jit(solution)/shard_map/pallas_call | solution.py:351
  19.9 0.6 %copy.7 = f32[2,4,2048]{2,1,0:T(4,128)} copy(f32[2,4,2048]{2,1,0:T(4,128)S(1)} %shard_map.55) | data formatting | bytes 131072
